TPU v7x, 256 devices: a whole 4x4x8 slice. The times are simulated.
256 devices in a mesh: wide: 32 (over z, y), slab: 8 (over x, core).
Axes of the slice: x: 4, y: 4, z: 8, core: 2. Of those that a mesh axis runs over, the one named last changes fastest.
Arguments:
- thermal_state: float32 [32, 128, 32, 1024], P('wide', 'slab'), may hold values from -5 to 5
- thermal_spreading_rate: bfloat16 [32, 128, 32, 1024], P('wide', 'slab'), may hold values from 0.5 to 1.5
- flow_speed_vector: bfloat16 [3, 32, 128, 32, 1024], P(None, 'wide', 'slab'), may hold values from -0.796875 to 0.796875
- interface_guess: float32 [32, 2048], P('wide', 'slab'), may hold values from -4 to 4
- partner_facing_rows: int32 [32, 2048], P('wide', 'slab'), may hold values from 0 to 2047, each once within a row
- mismatch_change_matrix: float32 [32, 2048, 128], P('wide', 'slab'), may hold values from -5 to 5
- output_change_matrix: float32 [32, 2048, 128], P('wide', 'slab'), may hold values from -1.8 to 1.8
Outputs:
- temperature_out: float32 [32, 128, 32, 1024], P('wide', 'slab')
- updated_interface_guess: float32 [32, 2048], P('wide', 'slab')
- unitary_basis_factor: float32 [32, 2048, 128], P('wide', 'slab')
Inputs may be any that keep to these rules, and one draw needn't show every extreme that they name: `partner_facing_rows`: each partition's rows of matching are a permutation of its partner's interface rows.
All inputs are finite; a program needn't handle non-finite values.
Results may differ from a plain program's by a relative error of at most 0.0003.
Values may be sent and summed in bfloat16 or wider, within the bound.
No kernel may reach another device: no remote copies, remote signals or barrier semaphores. Data moves between devices by JAX's collectives and lax.ppermute only.
A program may use at most 64 MiB of HBM per device.

v0:
```python
import math
import jax
import jax.numpy as jnp
from jax import lax
from jax.sharding import PartitionSpec as P

INTERFACE_STRIP = 64
SWEEPS = 4
STEP_SIZE = 0.11


def padded(cells, sides, width):
    for axis, dim in sides:
        count = lax.axis_size(axis)
        ends = count - 1
        head = lax.slice_in_dim(cells, 0, width, axis=dim)
        tail = lax.slice_in_dim(cells, cells.shape[dim] - width, cells.shape[dim], axis=dim)
        cells = jnp.concatenate(
            [
                lax.ppermute(tail, axis, [(i, (i + 1) % count) for i in range(ends)]),
                cells,
                lax.ppermute(head, axis, [((i + 1) % count, i) for i in range(ends)]),
            ],
            axis=dim,
        )
    return cells


def partner(value, axis, stride):
    mask = 2**stride
    pairs = [(source, source ^ mask) for source in range(lax.axis_size(axis))]
    return lax.ppermute(value, axis, pairs)


def surround_wrapper(block_rows, mirror_layer):
    bottom = jnp.zeros((block_rows.shape[0], 1, block_rows.shape[2]), block_rows.dtype)
    stacked = jnp.concatenate([bottom, block_rows, mirror_layer[:, None, :]], axis=1)
    return jnp.pad(stacked, ((0, 0), (0, 0), (1, 1)))


def march_forward(bordered_array, diffuse_subdomain, subdomain_flow_speed):
    centre = bordered_array[1:-1, 1:-1, 1:-1]
    plus_first = bordered_array[2:, 1:-1, 1:-1]
    minus_first = bordered_array[:-2, 1:-1, 1:-1]
    plus_second = bordered_array[1:-1, 2:, 1:-1]
    minus_second = bordered_array[1:-1, :-2, 1:-1]
    plus_third = bordered_array[1:-1, 1:-1, 2:]
    minus_third = bordered_array[1:-1, 1:-1, :-2]
    spread = (
        plus_first
        + minus_first
        + plus_second
        + minus_second
        + plus_third
        + minus_third
        - 6.0 * centre
    )
    carried = 0.5 * (
        subdomain_flow_speed[0].astype(jnp.float32) * (plus_first - minus_first)
        + subdomain_flow_speed[1].astype(jnp.float32) * (plus_second - minus_second)
        + subdomain_flow_speed[2].astype(jnp.float32) * (plus_third - minus_third)
    )
    return centre + STEP_SIZE * (diffuse_subdomain.astype(jnp.float32) * spread - carried)


def shards(
    thermal_state,
    thermal_spreading_rate,
    flow_speed_vector,
    interface_guess,
    partner_facing_rows,
    mismatch_change_matrix,
    output_change_matrix,
):
    subdomain_thermal_state = thermal_state[0]
    diffuse_subdomain = thermal_spreading_rate[0]
    subdomain_flow_speed = flow_speed_vector[:, 0]
    layer_stack = subdomain_thermal_state.shape[0]
    vertical_extent = subdomain_thermal_state.shape[1]
    rows_dev = interface_guess.shape[1]
    mirror_layer = jnp.repeat(interface_guess[0].reshape(layer_stack, -1), INTERFACE_STRIP, axis=1)
    panel = mismatch_change_matrix[0]
    gram_local = lax.dot_general(
        panel,
        panel,
        (((0,), (0,)), ((), ())),
        precision=lax.Precision.HIGHEST,
        preferred_element_type=jnp.float32,
    )
    ghost_padded = jnp.pad(mirror_layer, ((1, 1), (0, 0)))
    for sweep in range(SWEEPS):
        widened_array = padded(subdomain_thermal_state, (("slab", 0),), 1)
        subdomain_thermal_state = march_forward(
            surround_wrapper(widened_array, ghost_padded), diffuse_subdomain, subdomain_flow_speed
        )
    face_means = jnp.mean(
        subdomain_thermal_state[:, vertical_extent - 1, :].reshape(
            layer_stack, -1, INTERFACE_STRIP
        ),
        axis=2,
    )
    face_means = face_means.reshape(1, rows_dev)
    top_bit = lax.axis_size("wide").bit_length() - 2
    partner_own = partner(face_means, "wide", top_bit)
    partner_all = lax.all_gather(partner_own, "slab", axis=1, tiled=True)
    tilde = jnp.take(partner_all[0], partner_facing_rows[0], axis=0)
    resid = tilde - interface_guess[0]
    proj_local = jnp.dot(
        resid, panel, precision=lax.Precision.HIGHEST, preferred_element_type=jnp.float32
    )
    gram_matrix, projection = lax.psum((gram_local, proj_local), ("wide", "slab"))
    lower_factor = jnp.linalg.cholesky(gram_matrix)
    half_solve = lax.linalg.triangular_solve(
        lower_factor, projection[:, None], left_side=True, lower=True
    )
    coefficients = -lax.linalg.triangular_solve(
        lower_factor, half_solve, left_side=True, lower=True, transpose_a=True
    )[:, 0]
    update = jnp.dot(
        output_change_matrix[0],
        coefficients,
        precision=lax.Precision.HIGHEST,
        preferred_element_type=jnp.float32,
    )
    updated_interface_guess = tilde + update
    total_rows = rows_dev * lax.axis_size("slab") * lax.axis_size("wide")
    scaled = lax.linalg.triangular_solve(
        lower_factor, panel, left_side=False, lower=True, transpose_a=True
    )
    unitary_basis_factor = math.sqrt(total_rows) * scaled
    return (
        subdomain_thermal_state[None],
        updated_interface_guess[None],
        unitary_basis_factor[None],
    )


def solution(mesh):
    return jax.shard_map(
        shards,
        mesh=mesh,
        in_specs=(
            P("wide", "slab", None, None),
            P("wide", "slab", None, None),
            P(None, "wide", "slab", None, None),
            P("wide", "slab"),
            P("wide", "slab"),
            P("wide", "slab", None),
            P("wide", "slab", None),
        ),
        out_specs=(P("wide", "slab", None, None), P("wide", "slab"), P("wide", "slab", None)),
        check_vma=False,
    )
```

profile of v0, /device:TPU:1, one launch (start us, length us, event | category | flops | bytes accessed | tf_op | source)
XLA Modules:
  0.0 438.8 jit_solution(339822084845978649)
XLA Ops:
  8.2 5.1 %collective-permute-start = (f32[1,32,1024]{2,1,0:T(8,128)S(1)}, f32[1,32,1024]{2,1,0:T(8,128)S(1)}, u32[]{:S(2)}, u32[]{:S(2)}) collective-permute-start(f32[1,32,1024]{2,1,0:T(8,128)S(1)} %get-tuple-element.16), channel_id=1, source_target_pairs={{1,0},{2,1},{3,2},{4,3},{5,4},{6,5},{7,6},{9,8},{10,9},{11,10},{12... | collective-permute-start | bytes 393224 | tf_op jit(solution)/shard_map/ppermute | solution.py:22
  13.4 1.9 collective-permute-start.1
  17.6 1.3 reduce.11
  19.3 237.0 %all-reduce.11.cloned.1.call-done = f32[128,128]{0,1:T(8,128)} async-done(((f32[128,128]{0,1:T(8,128)}), f32[128,128]{0,1:T(8,128)}) %all-reduce.11.cloned.1.call-update) | async-done | bytes 65552 | tf_op jit(solution)/shard_map/psum | solution.py:111
  257.9 2.3 pad_maximum_fusion.3
  260.7 7.0 %fusion.2 = f32[16,32,1024]{2,1,0:T(8,128)S(1)} fusion(f32[16,32,1024]{2,1,0:T(8,128)} %bitcast.90, f32[18,34,1024]{2,1,0:T(8,128)S(1)} %pad_maximum_fusion.3, f32[1,32,1024]{2,1,0:T(8,128)S(1)} %collective-permute-done, f32[1,32,1024]{2,1,0:T(8,128)S(1)} %copy-done.11, f32[18,1,1024]{2,1,0:T(1,128)S(1)} %broadcast_in_dim.30, ...), kind=kLoop, calls=%fused_computation.35 | loop fusion | flops 18874368 | bytes 11231232 | tf_op jit(solution)/shard_map/add | solution.py:63
  267.8 1.3 copy-done.4
  269.8 1.9 collective-permute-start.2
  271.7 3.6 collective-permute-start.3
  276.0 12.5 %cholesky.16 = f32[128,128]{1,0:T(8,128)S(1)} custom-call(f32[128,128]{1,0:T(8,128)} %fusion.45), custom_call_target="Cholesky" | custom-call | tf_op jit(solution)/shard_map/jit(cholesky)/cholesky | solution.py:112
  288.6 2.3 pad_maximum_fusion.2
  291.1 4.6 %fusion.5 = f32[16,32,1024]{2,1,0:T(8,128)S(1)} fusion(f32[16,32,1024]{2,1,0:T(8,128)S(1)} %copy-done.5, f32[18,34,1024]{2,1,0:T(8,128)S(1)} %pad_maximum_fusion.2, f32[1,32,1024]{2,1,0:T(8,128)S(1)} %collective-permute-done.2, f32[1,32,1024]{2,1,0:T(8,128)} %collective-permute-done.3, f32[18,1,1024]{2,1,0:T(1,128)S(1)} %broadcast_in_dim.30, ...), kind=kLoop, calls=%fused_computation.38 | loop fusion | flops 18874368 | bytes 11231232 | tf_op jit(solution)/shard_map/add | solution.py:63
  295.8 1.9 collective-permute-start.4
  297.7 3.8 collective-permute-start.5
  304.0 5.4 %fusion.8 = f32[16,32,1024]{2,1,0:T(8,128)S(1)} fusion(f32[16,32,1024]{2,1,0:T(8,128)S(1)} %fusion.5, f32[18,34,1024]{2,1,0:T(8,128)S(1)} %pad_maximum_fusion.1, f32[1,32,1024]{2,1,0:T(8,128)S(1)} %collective-permute-done.4, f32[1,32,1024]{2,1,0:T(8,128)S(1)} %collective-permute-done.5, f32[18,1,1024]{2,1,0:T(1,128)S(1)} %broadcast_in_dim.30, ...), kind=kLoop, calls=%fused_computation.41 | loop fusion | flops 18874368 | bytes 11231232 | tf_op jit(solution)/shard_map/add | solution.py:63
  311.4 1.9 collective-permute-start.6
  313.3 4.4 collective-permute-start.7
  319.0 10.6 %custom-call.10 = f32[1,128,128]{1,2,0:T(8,128)S(1)} custom-call(f32[1,128,128]{2,1,0:T(8,128)} %fusion.41), custom_call_target="InvertDiagBlocksLowerTriangular" | custom-call | tf_op jit(solution)/shard_map/triangular_solve | solution.py:116
  329.7 2.3 pad_maximum_fusion
  332.2 4.6 %fusion.11 = f32[16,32,1024]{2,1,0:T(8,128)S(1)} fusion(f32[16,32,1024]{2,1,0:T(8,128)S(1)} %copy-done.3, f32[18,34,1024]{2,1,0:T(8,128)S(1)} %pad_maximum_fusion, f32[1,32,1024]{2,1,0:T(8,128)S(1)} %collective-permute-done.6, f32[1,32,1024]{2,1,0:T(8,128)} %collective-permute-done.7, f32[18,1,1024]{2,1,0:T(1,128)S(1)} %broadcast_in_dim.30, ...), kind=kLoop, calls=%fused_computation.44 | loop fusion | flops 18874368 | bytes 11231232 | tf_op jit(solution)/shard_map/add | solution.py:63
  340.6 4.4 %collective-permute-done.8 = f32[1,256]{1,0:T(1,128)S(1)} collective-permute-done((f32[1,256]{1,0:T(1,128)S(1)}, f32[1,256]{1,0:T(1,128)S(1)}, u32[]{:S(2)}, u32[]{:S(2)}) %collective-permute-start.8) | collective-permute-done | bytes 1056 | tf_op jit(solution)/shard_map/ppermute | solution.py:32
  345.0 10.1 %all_gather.3 = f32[1,2048]{1,0:T(1,128)S(1)} all-gather(f32[1,256]{1,0:T(1,128)S(1)} %collective-permute-done.8), channel_id=1, replica_groups=mesh['wide'=32,'slab'=8] {'slab'}, dimensions={1}, use_global_device_ids=true | all-gather | bytes 9216 | tf_op jit(solution)/shard_map/all_gather | solution.py:105
  355.1 1.7 gather_fusion
  357.0 73.7 %psum.15 = f32[128]{0:T(128)S(1)} all-reduce(f32[128]{0:T(128)S(1)} %convolution_bitcast_fusion.2), channel_id=1, replica_groups=mesh['wide'=32,'slab'=8] {'wide','slab'}, use_global_device_ids=true, to_apply=%region_4.5 | all-reduce | flops 128 | bytes 1024 | tf_op jit(solution)/shard_map/psum | solution.py:111
  (78 shorter events, 18.4 us)
Async XLA Ops:
  7.2 8.2 %copy-start = (f32[1,256,128]{2,1,0:T(8,128)S(1)}, f32[1,256,128]{2,1,0:T(8,128)}, u32[]{:S(2)}) copy-start(f32[1,256,128]{2,1,0:T(8,128)} %param.12) | copy-start | bytes 393220
  7.2 249.1 %all-reduce.11.cloned.1.call-start = ((), (), s32[]{:S(2)}) async-start(), calls=%async_computation | async-start | bytes 131072 | tf_op jit(solution)/shard_map/psum | solution.py:111
  8.2 249.0 %collective-permute-start = (f32[1,32,1024]{2,1,0:T(8,128)S(1)}, f32[1,32,1024]{2,1,0:T(8,128)S(1)}, u32[]{:S(2)}, u32[]{:S(2)}) collective-permute-start(f32[1,32,1024]{2,1,0:T(8,128)S(1)} %get-tuple-element.16), channel_id=1, source_target_pairs={{1,0},{2,1},{3,2},{4,3},{5,4},{6,5},{7,6},{9,8},{10,9},{11,10},{12... | collective-permute-start | bytes 393224 | tf_op jit(solution)/shard_map/ppermute | solution.py:22
  13.4 243.8 %collective-permute-start.1 = (f32[1,32,1024]{2,1,0:T(8,128)S(1)}, f32[1,32,1024]{2,1,0:T(8,128)S(1)}, u32[]{:S(2)}, u32[]{:S(2)}) collective-permute-start(f32[1,32,1024]{2,1,0:T(8,128)S(1)} %get-tuple-element.15), channel_id=1, source_target_pairs={{0,1},{1,2},{2,3},{3,4},{4,5},{5,6},{6,7},{8,9},{9,10},{10,11},{11... | collective-permute-start | bytes 393224 | tf_op jit(solution)/shard_map/ppermute | solution.py:20
  257.9 2.6 copy-start.1
  257.9 2.8 copy-start.6
  257.9 2.8 copy-start.11
  260.7 14.6 %copy-start.12 = (f32[128,128]{0,1:T(8,128)S(1)}, f32[128,128]{0,1:T(8,128)}, u32[]{:S(2)}) copy-start(f32[128,128]{0,1:T(8,128)} %all-reduce.11.cloned.1.call-done) | copy-start | bytes 196612
  269.8 18.8 %collective-permute-start.2 = (f32[1,32,1024]{2,1,0:T(8,128)}, f32[1,32,1024]{2,1,0:T(8,128)S(1)}, u32[]{:S(2)}, u32[]{:S(2)}) collective-permute-start(f32[1,32,1024]{2,1,0:T(8,128)} %get-tuple-element.14), channel_id=1, source_target_pairs={{1,0},{2,1},{3,2},{4,3},{5,4},{6,5},{7,6},{9,8},{10,9},{11,10},{12... | collective-permute-start | bytes 393224 | tf_op jit(solution)/shard_map/ppermute | solution.py:22
  271.7 16.9 %collective-permute-start.3 = (f32[1,32,1024]{2,1,0:T(8,128)}, f32[1,32,1024]{2,1,0:T(8,128)}, u32[]{:S(2)}, u32[]{:S(2)}) collective-permute-start(f32[1,32,1024]{2,1,0:T(8,128)} %get-tuple-element.13), channel_id=1, source_target_pairs={{0,1},{1,2},{2,3},{3,4},{4,5},{5,6},{6,7},{8,9},{9,10},{10,11},{11... | collective-permute-start | bytes 393224 | tf_op jit(solution)/shard_map/ppermute | solution.py:20
  288.6 13.0 %copy-start.13 = (f32[128,128]{1,0:T(8,128)}, f32[128,128]{1,0:T(8,128)S(1)}, u32[]{:S(2)}) copy-start(f32[128,128]{1,0:T(8,128)S(1)} %cholesky.16) | copy-start | bytes 196612
  288.6 2.3 copy-start.5
  288.6 2.5 copy-start.7
  295.8 6.4 %collective-permute-start.4 = (f32[1,32,1024]{2,1,0:T(8,128)S(1)}, f32[1,32,1024]{2,1,0:T(8,128)S(1)}, u32[]{:S(2)}, u32[]{:S(2)}) collective-permute-start(f32[1,32,1024]{2,1,0:T(8,128)S(1)} %get-tuple-element.12), channel_id=1, source_target_pairs={{1,0},{2,1},{3,2},{4,3},{5,4},{6,5},{7,6},{9,8},{10,9},{11,10},{12... | collective-permute-start | bytes 393224 | tf_op jit(solution)/shard_map/ppermute | solution.py:22
  297.7 5.6 %collective-permute-start.5 = (f32[1,32,1024]{2,1,0:T(8,128)S(1)}, f32[1,32,1024]{2,1,0:T(8,128)S(1)}, u32[]{:S(2)}, u32[]{:S(2)}) collective-permute-start(f32[1,32,1024]{2,1,0:T(8,128)S(1)} %get-tuple-element.11), channel_id=1, source_target_pairs={{0,1},{1,2},{2,3},{3,4},{4,5},{5,6},{6,7},{8,9},{9,10},{10,11},{11... | collective-permute-start | bytes 393224 | tf_op jit(solution)/shard_map/ppermute | solution.py:20
  304.0 13.7 %copy-start.14 = (f32[128,128]{1,0:T(8,128)S(1)}, f32[128,128]{1,0:T(8,128)}, u32[]{:S(2)}) copy-start(f32[128,128]{1,0:T(8,128)} %copy-done.13) | copy-start | bytes 196612
  311.4 18.2 %collective-permute-start.6 = (f32[1,32,1024]{2,1,0:T(8,128)}, f32[1,32,1024]{2,1,0:T(8,128)S(1)}, u32[]{:S(2)}, u32[]{:S(2)}) collective-permute-start(f32[1,32,1024]{2,1,0:T(8,128)} %get-tuple-element.10), channel_id=1, source_target_pairs={{1,0},{2,1},{3,2},{4,3},{5,4},{6,5},{7,6},{9,8},{10,9},{11,10},{12... | collective-permute-start | bytes 393224 | tf_op jit(solution)/shard_map/ppermute | solution.py:22
  313.3 16.3 %collective-permute-start.7 = (f32[1,32,1024]{2,1,0:T(8,128)}, f32[1,32,1024]{2,1,0:T(8,128)}, u32[]{:S(2)}, u32[]{:S(2)}) collective-permute-start(f32[1,32,1024]{2,1,0:T(8,128)} %get-tuple-element.9), channel_id=1, source_target_pairs={{0,1},{1,2},{2,3},{3,4},{4,5},{5,6},{6,7},{8,9},{9,10},{10,11},{11... | collective-permute-start | bytes 393224 | tf_op jit(solution)/shard_map/ppermute | solution.py:20
  329.6 2.3 copy-start.3
  329.7 2.5 copy-start.8
  338.2 18.6 %copy-start.16 = (s32[1,256]{1,0:T(1,128)S(1)}, s32[1,256]{1,0:T(1,128)}, u32[]{:S(2)}) copy-start(s32[1,256]{1,0:T(1,128)} %param.11) | copy-start | bytes 3076
  338.2 18.6 %copy-start.17 = (f32[1,256]{1,0:T(1,128)S(1)}, f32[1,256]{1,0:T(1,128)}, u32[]{:S(2)}) copy-start(f32[1,256]{1,0:T(1,128)} %param.10) | copy-start | bytes 3076
  338.2 92.9 %copy-start.15 = (f32[1,256,128]{2,1,0:T(8,128)S(1)}, f32[1,256,128]{2,1,0:T(8,128)}, u32[]{:S(2)}) copy-start(f32[1,256,128]{2,1,0:T(8,128)} %param.13) | copy-start | bytes 393220
  338.6 6.4 %collective-permute-start.8 = (f32[1,256]{1,0:T(1,128)S(1)}, f32[1,256]{1,0:T(1,128)S(1)}, u32[]{:S(2)}, u32[]{:S(2)}) collective-permute-start(f32[1,256]{1,0:T(1,128)S(1)} %div.18), channel_id=1, source_target_pairs={{0,128},{8,136},{16,144},{24,152},{32,160},{40,168},{48,176},{56,1... | collective-permute-start | bytes 3080 | tf_op jit(solution)/shard_map/ppermute | solution.py:32
  (4 other events, 4.6 us)
Sparse Core Ops, SparseCore 0:
  16.5 239.7 all-reduce.10
where the time goes:
time: 439 us
  waiting for transfers between devices  242 us (55%)
  blocking collectives  83.8 us (19%)
  other arithmetic  57.7 us (13%)
  starting transfers between devices  25.5 us (6%)
  between operations  14.5 us (3%)
  local copies, waits for them, and re-layouts  12.7 us (3%)
    psum x1, waiting for transfers between devices, shards(): lax.psum((gram_local, proj_local), ('wide', 'slab'))  237 us
    psum x1, blocking collectives, shards(): lax.psum((gram_local, proj_local), ('wide', 'slab'))  73.7 us
    add x4, other arithmetic, march_forward(): centre + STEP_SIZE * (diffuse_subdomain.astype(jnp.float32) * spread - ca...  21.7 us
    ppermute x4, starting transfers between devices, padded(): lax.ppermute(tail, axis, [(i, (i + 1) % count) for i in range(ends)])  13.7 us
    another operation x3, other arithmetic, shards(): lower_factor = jnp.linalg.cholesky(gram_matrix)  13.2 us
    another operation x2, other arithmetic, shards(): lax.linalg.triangular_solve(lower_factor, half_solve, left_side=True, low...  11.9 us
    ppermute x4, starting transfers between devices, padded(): lax.ppermute(head, axis, [((i + 1) % count, i) for i in range(ends)])  10.9 us
    all_gather x1, blocking collectives, shards(): partner_all = lax.all_gather(partner_own, 'slab', axis=1, tiled=True)  10.1 us
  transfers between devices with their start and end apart: 10, of which 3 were waited for; matrix products, arithmetic and copies ran while one was open for 7% of the time, Pallas kernels for 0%

commit v1 on v0

--- a/solution.py
+++ b/solution.py
@@ -102,7 +102,9 @@
     face_means = face_means.reshape(1, rows_dev)
     top_bit = lax.axis_size("wide").bit_length() - 2
     partner_own = partner(face_means, "wide", top_bit)
-    partner_all = lax.all_gather(partner_own, "slab", axis=1, tiled=True)
+    partner_all = jnp.concatenate(
+        lax.all_to_all(jnp.stack([partner_own] * lax.axis_size("slab")), "slab", 0, 0), axis=1
+    )
     tilde = jnp.take(partner_all[0], partner_facing_rows[0], axis=0)
     resid = tilde - interface_guess[0]
     proj_local = jnp.dot(

time: 439 us -> 417 us (0.950)
  waiting for transfers between devices: 242 us -> 224 us
  blocking collectives: 83.8 us -> 75.5 us
  starting transfers between devices: 25.5 us -> 30.7 us
    psum x1, waiting for transfers between devices: 237 us -> 219 us  [shards(): lax.psum((gram_local, proj_local), ('wide', 'slab'))]
    all_gather x1 -> x0, blocking collectives: 10.1 us -> none  [shards(): partner_all = lax.all_gather(partner_own, 'slab', axis=1, tiled=True)]
    all_to_all x0 -> x1, starting transfers between devices: none -> 5.69 us  [shards(): lax.all_to_all(jnp.stack([partner_own] * lax.axis_size('slab')), 'slab',...]
    ppermute x1, waiting for transfers between devices: 4.4 us -> 0.01 us  [partner(): return lax.ppermute(value, axis, pairs)]
  transfers between devices with their start and end apart: 10 -> 11, of which waited for: 3 -> 3; matrix products, arithmetic and copies ran while one was open for 7% -> 10% of each run, Pallas kernels for 0% -> 0%
where the time goes in v1:
time: 417 us; the launch traced here: 416 us
  waiting for transfers between devices  224 us (54%)
  blocking collectives  75.5 us (18%)
  other arithmetic  56.2 us (13%)
  starting transfers between devices  30.7 us (7%)
  between operations  14.5 us (3%)
  local copies, waits for them, and re-layouts  13.4 us (3%)
    psum x1, waiting for transfers between devices, shards(): lax.psum((gram_local, proj_local), ('wide', 'slab'))  219 us
    psum x1, blocking collectives, shards(): lax.psum((gram_local, proj_local), ('wide', 'slab'))  75.5 us
    add x4, other arithmetic, march_forward(): centre + STEP_SIZE * (diffuse_subdomain.astype(jnp.float32) * spread - ca...  21.7 us
    another operation x3, other arithmetic, shards(): lower_factor = jnp.linalg.cholesky(gram_matrix)  13.2 us
    ppermute x4, starting transfers between devices, padded(): lax.ppermute(tail, axis, [(i, (i + 1) % count) for i in range(ends)])  12.5 us
    ppermute x4, starting transfers between devices, padded(): lax.ppermute(head, axis, [((i + 1) % count, i) for i in range(ends)])  11.4 us
    another operation x2, other arithmetic, shards(): lax.linalg.triangular_solve(lower_factor, half_solve, left_side=True, low...  10.5 us
  transfers between devices with their start and end apart: 11, of which 3 were waited for; matrix products, arithmetic and copies ran while one was open for 10% of the time, Pallas kernels for 0%

profile of v1, /device:TPU:1, one launch (start us, length us, event | category | flops | bytes accessed | tf_op | source)
XLA Modules:
  0.0 416.2 jit_solution(12706895130356017373)
XLA Ops:
  8.2 5.1 %collective-permute-start = (f32[1,32,1024]{2,1,0:T(8,128)S(1)}, f32[1,32,1024]{2,1,0:T(8,128)S(1)}, u32[]{:S(2)}, u32[]{:S(2)}) collective-permute-start(f32[1,32,1024]{2,1,0:T(8,128)S(1)} %get-tuple-element.16), channel_id=1, source_target_pairs={{1,0},{2,1},{3,2},{4,3},{5,4},{6,5},{7,6},{9,8},{10,9},{11,10},{12... | collective-permute-start | bytes 393224 | tf_op jit(solution)/shard_map/ppermute | solution.py:22
  13.4 1.9 collective-permute-start.1
  16.9 1.3 reduce.11
  19.3 2.3 pad_maximum_fusion.3
  22.1 7.0 %fusion.2 = f32[16,32,1024]{2,1,0:T(8,128)S(1)} fusion(f32[16,32,1024]{2,1,0:T(8,128)} %bitcast.91, f32[18,34,1024]{2,1,0:T(8,128)S(1)} %pad_maximum_fusion.3, f32[1,32,1024]{2,1,0:T(8,128)S(1)} %collective-permute-done, f32[1,32,1024]{2,1,0:T(8,128)S(1)} %copy-done.11, f32[18,1,1024]{2,1,0:T(1,128)S(1)} %broadcast_in_dim.30, ...), kind=kLoop, calls=%fused_computation.35 | loop fusion | flops 18874368 | bytes 11231232 | tf_op jit(solution)/shard_map/add | solution.py:63
  29.1 1.3 copy-done.2
  31.2 2.4 collective-permute-start.2
  33.6 3.2 collective-permute-start.3
  37.3 219.0 %all-reduce.11.cloned.1.call-done = f32[128,128]{0,1:T(8,128)} async-done(((f32[128,128]{0,1:T(8,128)}), f32[128,128]{0,1:T(8,128)}) %all-reduce.11.cloned.1.call-update) | async-done | bytes 65552 | tf_op jit(solution)/shard_map/psum | solution.py:113
  257.3 2.3 pad_maximum_fusion.2
  259.8 4.7 %fusion.5 = f32[16,32,1024]{2,1,0:T(8,128)S(1)} fusion(f32[16,32,1024]{2,1,0:T(8,128)S(1)} %copy-done.3, f32[18,34,1024]{2,1,0:T(8,128)S(1)} %pad_maximum_fusion.2, f32[1,32,1024]{2,1,0:T(8,128)S(1)} %collective-permute-done.2, f32[1,32,1024]{2,1,0:T(8,128)} %collective-permute-done.3, f32[18,1,1024]{2,1,0:T(1,128)S(1)} %broadcast_in_dim.30, ...), kind=kLoop, calls=%fused_computation.38 | loop fusion | flops 18874368 | bytes 11231232 | tf_op jit(solution)/shard_map/add | solution.py:63
  266.5 1.9 collective-permute-start.4
  268.4 3.8 collective-permute-start.5
  272.9 12.5 %cholesky.16 = f32[128,128]{1,0:T(8,128)S(1)} custom-call(f32[128,128]{1,0:T(8,128)} %fusion.45), custom_call_target="Cholesky" | custom-call | tf_op jit(solution)/shard_map/jit(cholesky)/cholesky | solution.py:114
  285.5 2.3 pad_maximum_fusion.1
  288.0 4.6 %fusion.8 = f32[16,32,1024]{2,1,0:T(8,128)S(1)} fusion(f32[16,32,1024]{2,1,0:T(8,128)S(1)} %copy-done.5, f32[18,34,1024]{2,1,0:T(8,128)S(1)} %pad_maximum_fusion.1, f32[1,32,1024]{2,1,0:T(8,128)S(1)} %collective-permute-done.4, f32[1,32,1024]{2,1,0:T(8,128)} %collective-permute-done.5, f32[18,1,1024]{2,1,0:T(1,128)S(1)} %broadcast_in_dim.30, ...), kind=kLoop, calls=%fused_computation.41 | loop fusion | flops 18874368 | bytes 11231232 | tf_op jit(solution)/shard_map/add | solution.py:63
  292.7 1.9 collective-permute-start.6
  294.6 3.6 collective-permute-start.7
  300.8 5.4 %fusion.11 = f32[16,32,1024]{2,1,0:T(8,128)S(1)} fusion(f32[16,32,1024]{2,1,0:T(8,128)S(1)} %fusion.8, f32[18,34,1024]{2,1,0:T(8,128)S(1)} %pad_maximum_fusion, f32[1,32,1024]{2,1,0:T(8,128)S(1)} %collective-permute-done.6, f32[1,32,1024]{2,1,0:T(8,128)S(1)} %collective-permute-done.7, f32[18,1,1024]{2,1,0:T(1,128)S(1)} %broadcast_in_dim.30, ...), kind=kLoop, calls=%fused_computation.44 | loop fusion | flops 18874368 | bytes 11231232 | tf_op jit(solution)/shard_map/add | solution.py:63
  309.8 9.8 %custom-call.10 = f32[1,128,128]{1,2,0:T(8,128)S(1)} custom-call(f32[1,128,128]{2,1,0:T(8,128)S(1)} %fusion.41), custom_call_target="InvertDiagBlocksLowerTriangular" | custom-call | tf_op jit(solution)/shard_map/triangular_solve | solution.py:118
  320.2 5.7 %all-to-all-start = ((f32[8,1,256]{2,1,0:T(1,128)}), f32[8,1,256]{2,1,0:T(1,128)S(1)}, u32[]{:S(2)}, u32[]{:S(2)}) async-start(f32[8,1,256]{2,1,0:T(1,128)} %stack.2), calls=%async_computation | async-start | bytes 16384 | tf_op jit(solution)/shard_map/all_to_all | solution.py:106
  327.0 3.5 all-to-all-done
  330.5 1.9 gather_fusion
  332.6 75.5 %psum.15 = f32[128]{0:T(128)S(1)} all-reduce(f32[128]{0:T(128)S(1)} %convolution_bitcast_fusion.2), channel_id=1, replica_groups=mesh['wide'=32,'slab'=8] {'wide','slab'}, use_global_device_ids=true, to_apply=%region_4.5 | all-reduce | flops 128 | bytes 1024 | tf_op jit(solution)/shard_map/psum | solution.py:113
  (76 shorter events, 18.7 us)
Async XLA Ops:
  7.2 8.2 %copy-start = (f32[1,256,128]{2,1,0:T(8,128)S(1)}, f32[1,256,128]{2,1,0:T(8,128)}, u32[]{:S(2)}) copy-start(f32[1,256,128]{2,1,0:T(8,128)} %param.12) | copy-start | bytes 393220
  7.2 249.1 %all-reduce.11.cloned.1.call-start = ((), (), s32[]{:S(2)}) async-start(), calls=%async_computation.1 | async-start | bytes 131072 | tf_op jit(solution)/shard_map/psum | solution.py:113
  8.2 10.4 %collective-permute-start = (f32[1,32,1024]{2,1,0:T(8,128)S(1)}, f32[1,32,1024]{2,1,0:T(8,128)S(1)}, u32[]{:S(2)}, u32[]{:S(2)}) collective-permute-start(f32[1,32,1024]{2,1,0:T(8,128)S(1)} %get-tuple-element.16), channel_id=1, source_target_pairs={{1,0},{2,1},{3,2},{4,3},{5,4},{6,5},{7,6},{9,8},{10,9},{11,10},{12... | collective-permute-start | bytes 393224 | tf_op jit(solution)/shard_map/ppermute | solution.py:22
  13.4 5.2 %collective-permute-start.1 = (f32[1,32,1024]{2,1,0:T(8,128)S(1)}, f32[1,32,1024]{2,1,0:T(8,128)S(1)}, u32[]{:S(2)}, u32[]{:S(2)}) collective-permute-start(f32[1,32,1024]{2,1,0:T(8,128)S(1)} %get-tuple-element.15), channel_id=1, source_target_pairs={{0,1},{1,2},{2,3},{3,4},{4,5},{5,6},{6,7},{8,9},{9,10},{10,11},{11... | collective-permute-start | bytes 393224 | tf_op jit(solution)/shard_map/ppermute | solution.py:20
  19.3 2.6 copy-start.1
  19.3 2.8 copy-start.6
  19.3 2.8 copy-start.11
  22.1 14.6 %copy-start.14 = (s32[1,256]{1,0:T(1,128)S(1)}, s32[1,256]{1,0:T(1,128)}, u32[]{:S(2)}) copy-start(s32[1,256]{1,0:T(1,128)} %param.11) | copy-start | bytes 3076
  29.1 1.3 copy-start.2
  31.2 226.1 %collective-permute-start.2 = (f32[1,32,1024]{2,1,0:T(8,128)}, f32[1,32,1024]{2,1,0:T(8,128)S(1)}, u32[]{:S(2)}, u32[]{:S(2)}) collective-permute-start(f32[1,32,1024]{2,1,0:T(8,128)} %get-tuple-element.14), channel_id=1, source_target_pairs={{1,0},{2,1},{3,2},{4,3},{5,4},{6,5},{7,6},{9,8},{10,9},{11,10},{12... | collective-permute-start | bytes 393224 | tf_op jit(solution)/shard_map/ppermute | solution.py:22
  33.6 223.7 %collective-permute-start.3 = (f32[1,32,1024]{2,1,0:T(8,128)}, f32[1,32,1024]{2,1,0:T(8,128)}, u32[]{:S(2)}, u32[]{:S(2)}) collective-permute-start(f32[1,32,1024]{2,1,0:T(8,128)} %get-tuple-element.13), channel_id=1, source_target_pairs={{0,1},{1,2},{2,3},{3,4},{4,5},{5,6},{6,7},{8,9},{9,10},{10,11},{11... | collective-permute-start | bytes 393224 | tf_op jit(solution)/shard_map/ppermute | solution.py:20
  257.2 2.3 copy-start.3
  257.3 2.5 copy-start.7
  259.8 12.5 %copy-start.12 = (f32[128,128]{0,1:T(8,128)S(1)}, f32[128,128]{0,1:T(8,128)}, u32[]{:S(2)}) copy-start(f32[128,128]{0,1:T(8,128)} %all-reduce.11.cloned.1.call-done) | copy-start | bytes 196612
  266.5 19.0 %collective-permute-start.4 = (f32[1,32,1024]{2,1,0:T(8,128)}, f32[1,32,1024]{2,1,0:T(8,128)S(1)}, u32[]{:S(2)}, u32[]{:S(2)}) collective-permute-start(f32[1,32,1024]{2,1,0:T(8,128)} %get-tuple-element.12), channel_id=1, source_target_pairs={{1,0},{2,1},{3,2},{4,3},{5,4},{6,5},{7,6},{9,8},{10,9},{11,10},{12... | collective-permute-start | bytes 393224 | tf_op jit(solution)/shard_map/ppermute | solution.py:22
  268.4 17.1 %collective-permute-start.5 = (f32[1,32,1024]{2,1,0:T(8,128)}, f32[1,32,1024]{2,1,0:T(8,128)}, u32[]{:S(2)}, u32[]{:S(2)}) collective-permute-start(f32[1,32,1024]{2,1,0:T(8,128)} %get-tuple-element.11), channel_id=1, source_target_pairs={{0,1},{1,2},{2,3},{3,4},{4,5},{5,6},{6,7},{8,9},{9,10},{10,11},{11... | collective-permute-start | bytes 393224 | tf_op jit(solution)/shard_map/ppermute | solution.py:20
  285.4 2.3 copy-start.5
  285.5 2.5 copy-start.8
  292.7 6.3 %collective-permute-start.6 = (f32[1,32,1024]{2,1,0:T(8,128)S(1)}, f32[1,32,1024]{2,1,0:T(8,128)S(1)}, u32[]{:S(2)}, u32[]{:S(2)}) collective-permute-start(f32[1,32,1024]{2,1,0:T(8,128)S(1)} %get-tuple-element.10), channel_id=1, source_target_pairs={{1,0},{2,1},{3,2},{4,3},{5,4},{6,5},{7,6},{9,8},{10,9},{11,10},{12... | collective-permute-start | bytes 393224 | tf_op jit(solution)/shard_map/ppermute | solution.py:22
  294.6 5.6 %collective-permute-start.7 = (f32[1,32,1024]{2,1,0:T(8,128)S(1)}, f32[1,32,1024]{2,1,0:T(8,128)S(1)}, u32[]{:S(2)}, u32[]{:S(2)}) collective-permute-start(f32[1,32,1024]{2,1,0:T(8,128)S(1)} %get-tuple-element.9), channel_id=1, source_target_pairs={{0,1},{1,2},{2,3},{3,4},{4,5},{5,6},{6,7},{8,9},{9,10},{10,11},{11... | collective-permute-start | bytes 393224 | tf_op jit(solution)/shard_map/ppermute | solution.py:20
  307.6 24.8 %copy-start.15 = (f32[1,256]{1,0:T(1,128)S(1)}, f32[1,256]{1,0:T(1,128)}, u32[]{:S(2)}) copy-start(f32[1,256]{1,0:T(1,128)} %param.10) | copy-start | bytes 3076
  307.6 100.9 %copy-start.13 = (f32[1,256,128]{2,1,0:T(8,128)S(1)}, f32[1,256,128]{2,1,0:T(8,128)}, u32[]{:S(2)}) copy-start(f32[1,256,128]{2,1,0:T(8,128)} %param.13) | copy-start | bytes 393220
  308.0 11.6 %collective-permute-start.8 = (f32[1,256]{1,0:T(1,128)S(1)}, f32[1,256]{1,0:T(1,128)S(1)}, u32[]{:S(2)}, u32[]{:S(2)}) collective-permute-start(f32[1,256]{1,0:T(1,128)S(1)} %div.18), channel_id=1, source_target_pairs={{0,128},{8,136},{16,144},{24,152},{32,160},{40,168},{48,176},{56,1... | collective-permute-start | bytes 3080 | tf_op jit(solution)/shard_map/ppermute | solution.py:32
  320.2 10.3 %all-to-all-start = ((f32[8,1,256]{2,1,0:T(1,128)}), f32[8,1,256]{2,1,0:T(1,128)S(1)}, u32[]{:S(2)}, u32[]{:S(2)}) async-start(f32[8,1,256]{2,1,0:T(1,128)} %stack.2), calls=%async_computation | async-start | bytes 16384 | tf_op jit(solution)/shard_map/all_to_all | solution.py:106
  (3 other events, 3.3 us)
Sparse Core Ops, SparseCore 0:
  16.5 239.7 all-reduce.10
